TPU v7x, 32 devices: a whole 2x2x4 slice. The times are simulated.
32 devices in a mesh: ctx: 8 (over z, x), head: 4 (over y, core).
Axes of the slice: x: 2, y: 2, z: 4, core: 2. Of those that a mesh axis runs over, the one named last changes fastest.
Arguments:
- qkv: bfloat16 [4096, 12288], P(('ctx', 'head')), may hold values from -26 to 26
- grad_out: bfloat16 [4096, 4096], P(('ctx', 'head')), may hold values from -6 to 6
- key_lists: int32 [32, 4], P('ctx'), may hold values from 0 to 31, as said below
- live_counts: int32 [32], P('ctx'), may hold values from 1 to 4
Outputs:
- grad_qkv: bfloat16 [4096, 12288], P(('ctx', 'head'))
Inputs may be any that keep to these rules, and one draw needn't show every extreme that they name: `key_lists`: each entry names a block whose index of ctx is within 2 of its query block's and which is not within one block of its query block; the 4 entries of a row differ. Over all 4 entries of all rows (live or not) of one index of ctx, the blocks named on any other index of ctx are at most 2 of its blocks, and this is reached.
All inputs are finite; a program needn't handle non-finite values.
Results may differ from a plain program's by a relative error of at most 0.008.
Values may be sent and summed in bfloat16 or wider, within the bound.
A program may use at most 192 MiB of HBM per device.

v0:
```python
import jax
import jax.numpy as jnp
from jax import lax
from jax.sharding import PartitionSpec as P

HD = 128
BLK = 128
SEARCHER_TILES = 4
DRAWN_TARGET_SET = 4
SPAN = 2
NAMED_TILE_LIMIT = 2


def extended_2(cells, sides, width):
    for axis, dim in sides:
        count = lax.axis_size(axis)
        ends = count - 1
        head = lax.slice_in_dim(cells, 0, width, axis=dim)
        tail = lax.slice_in_dim(cells, cells.shape[dim] - width, cells.shape[dim], axis=dim)
        cells = jnp.concatenate(
            [
                lax.ppermute(tail, axis, [(i, (i + 1) % count) for i in range(ends)]),
                cells,
                lax.ppermute(head, axis, [((i + 1) % count, i) for i in range(ends)]),
            ],
            axis=dim,
        )
    return cells


def from_behind(value, axis, steps):
    count = lax.axis_size(axis)
    initial, last = (max(0, -steps), min(count, count - steps))
    return lax.ppermute(value, axis, [(source, source + steps) for source in range(initial, last)])


def block_grads(query_part, grad_part, key_part, value_part, usable):
    scaling = HD ** (-0.5)
    tile_merits = (
        jnp.einsum("qhd,nkhd->hqnk", query_part, key_part, preferred_element_type=jnp.float32)
        * scaling
    )
    weight = usable.astype(jnp.float32)[None, None, :, None]
    masked = jnp.where(weight > 0.0, tile_merits, -1e30)
    highest = jnp.max(masked, axis=(2, 3), keepdims=True)
    powers = jnp.exp(masked - highest) * weight
    soft_weights = powers / jnp.sum(powers, axis=(2, 3), keepdims=True)
    grad_soft = jnp.einsum(
        "qhd,nkhd->hqnk", grad_part, value_part, preferred_element_type=jnp.float32
    )
    row_delta = jnp.sum(soft_weights * grad_soft, axis=(2, 3), keepdims=True)
    grad_scores = soft_weights * (grad_soft - row_delta)
    soft_low = soft_weights.astype(jnp.bfloat16)
    scores_low = grad_scores.astype(jnp.bfloat16)
    grad_values = jnp.einsum(
        "hqnk,qhd->nkhd", soft_low, grad_part, preferred_element_type=jnp.float32
    )
    grad_keys = (
        jnp.einsum("hqnk,qhd->nkhd", scores_low, query_part, preferred_element_type=jnp.float32)
        * scaling
    )
    grad_query = (
        jnp.einsum("hqnk,nkhd->qhd", scores_low, key_part, preferred_element_type=jnp.float32)
        * scaling
    )
    return (grad_query, jnp.stack([grad_keys, grad_values], axis=3))


def needed_blocks(list_rows, owner_shard):
    targets = owner_shard * SEARCHER_TILES + jnp.arange(SEARCHER_TILES, dtype=jnp.int32)
    matches = list_rows[:, :, None] == targets[None, None, :]
    return jnp.any(matches, axis=(0, 1))


def slot_numbers(needed):
    block_order = jnp.arange(SEARCHER_TILES, dtype=jnp.int32)
    earlier = block_order[None, :] < block_order[:, None]
    return jnp.sum(jnp.where(earlier & needed[None, :], 1, 0), axis=1).astype(jnp.int32)


def select_table(needed):
    slot_of = slot_numbers(needed)
    slot_range = jnp.arange(NAMED_TILE_LIMIT, dtype=jnp.int32)
    return (needed[None, :] & (slot_of[None, :] == slot_range[:, None])).astype(jnp.float32)


def shards(qkv, grad_out, key_lists, live_counts):
    merged, grad_rows = (
        lax.all_to_all(qkv, "head", split_axis=1, concat_axis=0, tiled=True),
        lax.all_to_all(grad_out, "head", split_axis=1, concat_axis=0, tiled=True),
    )
    row_count = merged.shape[0]
    head_count = grad_rows.shape[1] // HD
    pair_width = head_count * 2 * HD
    per_head = merged.reshape(row_count, head_count, 3, HD)
    query_rows = per_head[:, :, 0]
    pair_rows = per_head[:, :, 1:].reshape(row_count, pair_width)
    shard_index = lax.axis_index("ctx")
    total_blocks = SEARCHER_TILES * lax.axis_size("ctx")
    local_ids = shard_index * SEARCHER_TILES + jnp.arange(SEARCHER_TILES, dtype=jnp.int32)
    window = local_ids[:, None] - 1 + jnp.arange(3, dtype=jnp.int32)[None, :]
    window_ok = (window >= 0) & (window < total_blocks)
    listed_ok = jnp.arange(DRAWN_TARGET_SET, dtype=jnp.int32)[None, :] < live_counts[:, None]
    usable = jnp.concatenate([window_ok, listed_ok], axis=1)
    offsets = [offset for offset in range(-SPAN, SPAN + 1) if offset != 0]
    owner_tables = []
    rims = extended_2(pair_rows, (("ctx", 0),), BLK)
    pieces = [rims]
    rank_list = []
    own_blocks = pair_rows.reshape(SEARCHER_TILES, BLK, pair_width)
    for offset in offsets:
        wanted = needed_blocks(key_lists, shard_index + offset)
        rank_list.append(slot_numbers(wanted))
        theirs = from_behind(key_lists, "ctx", offset)
        owner_table = select_table(needed_blocks(theirs, shard_index))
        owner_tables.append(owner_table)
        outgoing = jnp.einsum(
            "st,tbf->sbf",
            owner_table.astype(jnp.bfloat16),
            own_blocks,
            preferred_element_type=jnp.float32,
        )
        outgoing = outgoing.astype(jnp.bfloat16).reshape(NAMED_TILE_LIMIT * BLK, pair_width)
        pieces.append(from_behind(outgoing, "ctx", -offset))
    extended = jnp.concatenate(pieces, axis=0)
    rank_table = jnp.stack(rank_list)
    gap_shard = key_lists // SEARCHER_TILES - shard_index
    block_in = key_lists % SEARCHER_TILES
    side_of = jnp.where(gap_shard < 0, gap_shard + SPAN, gap_shard + SPAN - 1)
    side_hit = side_of[:, :, None] == jnp.arange(2 * SPAN, dtype=jnp.int32)[None, None, :]
    block_hit = block_in[:, :, None] == jnp.arange(SEARCHER_TILES, dtype=jnp.int32)[None, None, :]
    rank_here = jnp.sum(
        jnp.where(side_hit[:, :, :, None] & block_hit[:, :, None, :], rank_table[None, None], 0),
        axis=(2, 3),
    )
    far_place = SEARCHER_TILES + 2 + side_of * NAMED_TILE_LIMIT + rank_here
    listed_place = jnp.where(gap_shard == 0, 1 + block_in, far_place)
    window_place = jnp.clip(window - shard_index * SEARCHER_TILES + 1, 0, SEARCHER_TILES + 1)
    places = jnp.concatenate([window_place, listed_place], axis=1)
    block_count = extended.shape[0] // BLK
    tile_ordinals = extended.reshape(block_count, BLK, head_count, 2, HD)
    query_blocks = query_rows.reshape(SEARCHER_TILES, BLK, head_count, HD)
    grad_blocks = grad_rows.reshape(SEARCHER_TILES, BLK, head_count, HD)

    def step(carry, inputs):
        query_part, grad_part, block_places, block_ok = inputs
        chosen = tile_ordinals[block_places]
        grad_query, grad_pairs = block_grads(
            query_part, grad_part, chosen[:, :, :, 0], chosen[:, :, :, 1], block_ok
        )
        return (carry, (grad_query, grad_pairs))

    carry_zero = jnp.zeros((), jnp.float32)
    carry_zero, outputs = lax.scan(step, carry_zero, (query_blocks, grad_blocks, places, usable))
    grad_query, pair_terms = outputs
    slot_total = pair_terms.shape[0] * pair_terms.shape[1]
    flat_terms = pair_terms.reshape(slot_total, BLK * pair_width)
    place_flat = places.reshape(slot_total)
    owner_hits = (place_flat[None, :] == jnp.arange(block_count, dtype=jnp.int32)[:, None]).astype(
        jnp.float32
    )
    totals = jnp.dot(
        owner_hits, flat_terms, precision=lax.Precision.HIGHEST, preferred_element_type=jnp.float32
    )
    totals = totals.reshape(block_count, BLK, pair_width)
    own_grads = totals[1 : SEARCHER_TILES + 1]
    for direction in (-1, 1):
        rim_rows = totals[0] if direction == -1 else totals[SEARCHER_TILES + 1]
        arrived = from_behind(rim_rows.astype(jnp.bfloat16), "ctx", direction).astype(
            rim_rows.dtype
        )
        target_block = SEARCHER_TILES - 1 if direction == -1 else 0
        own_grads = own_grads.at[target_block].add(arrived)
    for side_index, offset in enumerate(offsets):
        first_slot = SEARCHER_TILES + 2 + side_index * NAMED_TILE_LIMIT
        arrived = from_behind(totals[first_slot : first_slot + NAMED_TILE_LIMIT], "ctx", offset)
        own_grads = own_grads + jnp.einsum(
            "st,sbf->tbf", owner_tables[side_index], arrived, precision=lax.Precision.HIGHEST
        )
    own_grads = own_grads.reshape(SEARCHER_TILES, BLK, head_count, 2, HD)
    joined = jnp.concatenate([grad_query[:, :, :, None, :], own_grads], axis=3)
    joined = joined.astype(jnp.bfloat16).reshape(row_count, head_count * 3 * HD)
    return lax.all_to_all(joined, "head", split_axis=0, concat_axis=1, tiled=True)


def solution(mesh):
    placed = (P(("ctx", "head"), None), P(("ctx", "head"), None), P("ctx", None), P("ctx"))
    return jax.shard_map(
        shards, mesh=mesh, in_specs=placed, out_specs=P(("ctx", "head"), None), check_vma=False
    )
```

profile of v0, /device:TPU:0, one launch (start us, length us, event | category | flops | bytes accessed | tf_op | source)
XLA Modules:
  0.0 669.7 jit_solution(15242273154368790769)
XLA Ops:
  0.0 4.9 collective-permute-start.8
  5.0 3.4 collective-permute-start.6
  11.0 4.6 copy.138
  15.6 3.8 all-to-all-start
  24.3 32.0 %all-to-all-done = bf16[128,4,3072]{0,2,1:T(8,128)(2,1)S(1)} async-done(((bf16[128,4,3072]{0,2,1:T(8,128)(2,1)}), bf16[128,4,3072]{0,2,1:T(8,128)(2,1)S(1)}, u32[]{:S(2)}, u32[]{:S(2)}) %all-to-all-start) | async-done | bytes 3145760 | tf_op jit(solution)/shard_map/all_to_all | solution.py:89
  56.3 4.2 all-to-all-start.1
  60.6 15.6 %copy.139 = bf16[4,128,3072]{1,0,2:T(4,128)(2,1)} copy(bf16[4,128,3072]{1,2,0:T(8,128)(2,1)S(1)} %bitcast.205) | data formatting | bytes 6291456 | tf_op jit(solution)/shard_map/all_to_all | solution.py:89
  76.1 4.0 reshape.223
  86.0 5.5 collective-permute-start
  98.3 4.6 copy.143
  105.6 7.1 %collective-permute-start.3 = (bf16[256,2048]{1,0:T(8,128)(2,1)}, bf16[256,2048]{1,0:T(8,128)(2,1)}, u32[]{:S(2)}, u32[]{:S(2)}) collective-permute-start(bf16[256,2048]{1,0:T(8,128)(2,1)} %bitcast.34), channel_id=1, source_target_pairs={{0,8},{4,12},{8,16},{12,20},{16,24},{20,28},{1,9},{5,13},{9,17},{1... | collective-permute-start | bytes 3145736 | tf_op jit(solution)/shard_map/ppermute | solution.py:34
  115.3 4.1 collective-permute-start.5
  123.3 3.0 convolution_convert_fusion
  138.0 25.6 %collective-permute-done.5 = bf16[256,2048]{1,0:T(8,128)(2,1)} collective-permute-done((bf16[256,2048]{1,0:T(8,128)(2,1)}, bf16[256,2048]{1,0:T(8,128)(2,1)}, u32[]{:S(2)}, u32[]{:S(2)}) %collective-permute-start.5) | collective-permute-done | bytes 1048608 | tf_op jit(solution)/shard_map/ppermute | solution.py:34
  168.3 3.1 collective-permute-done.9
  172.4 12.6 %reshape.229 = bf16[14,128,8,2,128]{4,3,2,1,0:T(2,128)(2,1)} reshape(bf16[1792,2048]{1,0:T(8,128)(2,1)} %constant_dynamic-update-slice_fusion) | data formatting | bytes 14680064 | tf_op jit(solution)/shard_map/reshape | solution.py:141
  185.0 7.5 %copy.154 = bf16[14,128,8,2,128]{4,2,3,1,0:T(8,128)(2,1)} copy(bf16[14,128,8,2,128]{4,3,2,1,0:T(2,128)(2,1)} %reshape.229) | data formatting | bytes 14680064 | tf_op jit(solution)/shard_map/while | solution.py:154
  192.5 143.2 %while.14 = (s32[]{:T(128)}, bf16[4,128,8,128]{1,3,2,0:T(8,128)(2,1)S(1)}, f32[4,7,128,8,2,128]{5,4,3,2,1,0:T(2,128)}, s32[4,7]{1,0:T(4,128)S(1)}, bf16[14,128,8...) while((s32[]{:T(128)}, ...), condition=%wide.region_21.22_spmd, body=%wide.region_17.21_spmd.sunk | while | flops 1203894272 | bytes 104907184 | solution.py:154
  192.7 6.1 gather_fusion
  212.7 3.9 maximum_bitcast_fusion.2
  216.6 11.7 %copy_dynamic-update-slice_fusion.2 = f32[4,7,128,8,2,128]{5,4,3,2,1,0:T(2,128)} fusion(f32[4,7,128,8,2,128]{5,4,3,2,1,0:T(2,128)} %get-tuple-element.224, s32[]{:T(128)S(6)} %copy.226, f32[1,7,128,8,2,128]{5,2,1,3,4,0:T(8,128)} %maximum_bitcast_fusion.2), kind=kLoop, calls=%fused_computation.2.clone.1 | loop fusion | bytes 14680068 | tf_op jit(solution)/shard_map/while/body/jit(dynamic_update_index_in_dim)/dynamic_update_slice | solution.py:154
  228.3 6.1 gather_fusion
  248.3 3.9 maximum_bitcast_fusion.2
  252.2 11.8 %copy_dynamic-update-slice_fusion.2 = f32[4,7,128,8,2,128]{5,4,3,2,1,0:T(2,128)} fusion(f32[4,7,128,8,2,128]{5,4,3,2,1,0:T(2,128)} %get-tuple-element.224, s32[]{:T(128)S(6)} %copy.226, f32[1,7,128,8,2,128]{5,2,1,3,4,0:T(8,128)} %maximum_bitcast_fusion.2), kind=kLoop, calls=%fused_computation.2.clone.1 | loop fusion | bytes 14680068 | tf_op jit(solution)/shard_map/while/body/jit(dynamic_update_index_in_dim)/dynamic_update_slice | solution.py:154
  264.0 6.1 gather_fusion
  284.0 3.9 maximum_bitcast_fusion.2
  287.9 11.8 %copy_dynamic-update-slice_fusion.2 = f32[4,7,128,8,2,128]{5,4,3,2,1,0:T(2,128)} fusion(f32[4,7,128,8,2,128]{5,4,3,2,1,0:T(2,128)} %get-tuple-element.224, s32[]{:T(128)S(6)} %copy.226, f32[1,7,128,8,2,128]{5,2,1,3,4,0:T(8,128)} %maximum_bitcast_fusion.2), kind=kLoop, calls=%fused_computation.2.clone.1 | loop fusion | bytes 14680068 | tf_op jit(solution)/shard_map/while/body/jit(dynamic_update_index_in_dim)/dynamic_update_slice | solution.py:154
  299.7 6.1 gather_fusion
  319.7 3.9 maximum_bitcast_fusion.2
  323.7 11.7 %copy_dynamic-update-slice_fusion.2 = f32[4,7,128,8,2,128]{5,4,3,2,1,0:T(2,128)} fusion(f32[4,7,128,8,2,128]{5,4,3,2,1,0:T(2,128)} %get-tuple-element.224, s32[]{:T(128)S(6)} %copy.226, f32[1,7,128,8,2,128]{5,2,1,3,4,0:T(8,128)} %maximum_bitcast_fusion.2), kind=kLoop, calls=%fused_computation.2.clone.1 | loop fusion | bytes 14680068 | tf_op jit(solution)/shard_map/while/body/jit(dynamic_update_index_in_dim)/dynamic_update_slice | solution.py:154
  335.7 51.0 %reshape.231 = f32[28,262144]{1,0:T(8,128)} reshape(f32[4,7,128,8,2,128]{5,4,3,2,1,0:T(2,128)} %get-tuple-element.73) | data formatting | bytes 58720256 | tf_op jit(solution)/shard_map/reshape | solution.py:157
  386.7 25.8 %fusion.84 = (bf16[14,262144]{1,0:T(8,128)(2,1)}, f32[14,262144]{1,0:T(8,128)}) fusion(f32[28,262144]{1,0:T(8,128)} %reshape.231, s32[28]{0:T(128)S(1)} %copy-done.27), kind=kOutput, calls=%fused_computation.152 | convolution fusion | flops 1236795776 | bytes 51380336 | tf_op jit(solution)/shard_map/dot_general | solution.py:162
  412.4 15.1 %fusion.82 = (f32[2,262144]{1,0:T(2,128)}, f32[2,262144]{1,0:T(2,128)}, f32[2,262144]{1,0:T(2,128)}, f32[2,262144]{1,0:T(2,128)}) fusion(f32[14,262144]{1,0:T(8,128)} %get-tuple-element.145), kind=kLoop, calls=%fused_computation.150 | loop fusion | bytes 16777216 | tf_op jit(solution)/shard_map/slice | solution.py:176
  431.5 13.9 %slice_reduce_fusion = (bf16[262144]{0:T(1024)(128)(2,1)S(1)}, bf16[262144]{0:T(1024)(128)(2,1)S(1)}) fusion(bf16[14,262144]{1,0:T(8,128)(2,1)} %get-tuple-element.144), kind=kLoop, calls=%fused_computation.47 | loop fusion | bytes 2097152 | tf_op jit(solution)/shard_map/slice | solution.py:168
  447.9 7.5 %collective-permute-start.11 = (bf16[128,2048]{1,0:T(8,128)(2,1)}, bf16[128,2048]{1,0:T(8,128)(2,1)}, u32[]{:S(2)}, u32[]{:S(2)}) collective-permute-start(bf16[128,2048]{1,0:T(8,128)(2,1)} %convert_element_type.88), channel_id=1, source_target_pairs={{0,4},{4,8},{8,12},{12,16},{16,20},{20,24},{24,28},{1,5},{5,9},{9,... | collective-permute-start | bytes 1572872 | tf_op jit(solution)/shard_map/ppermute | solution.py:34
  456.7 13.2 %slice_reduce_fusion.2 = f32[262144]{0:T(1024)S(1)} fusion(f32[14,262144]{1,0:T(8,128)} %get-tuple-element.145), kind=kLoop, calls=%fused_computation.50 | loop fusion | bytes 2097152 | tf_op jit(solution)/shard_map/slice.64
  469.9 5.2 slice.140
  475.3 16.0 %collective-permute-done.10 = bf16[128,2048]{1,0:T(8,128)(2,1)S(1)} collective-permute-done((bf16[128,2048]{1,0:T(8,128)(2,1)S(1)}, bf16[128,2048]{1,0:T(8,128)(2,1)S(1)}, u32[]{:S(2)}, u32[]{:S(2)}) %collective-permute-start.10) | collective-permute-done | bytes 524320 | tf_op jit(solution)/shard_map/ppermute | solution.py:34
  492.1 57.7 %collective-permute-start.15 = (f32[2,128,2048]{2,0,1:T(2,128)}, f32[2,128,2048]{2,0,1:T(2,128)S(1)}, u32[]{:S(2)}, u32[]{:S(2)}) collective-permute-start(f32[2,128,2048]{2,0,1:T(2,128)} %bitcast.214), channel_id=1, source_target_pairs={{0,8},{4,12},{8,16},{12,20},{16,24},{20,28},{1,9},{5,13},{9,17},{1... | collective-permute-start | bytes 6291464 | tf_op jit(solution)/shard_map/ppermute | solution.py:34
  551.7 19.7 %scatter-add.6 = f32[4,128,2048]{2,0,1:T(4,128)} dynamic-update-slice(f32[4,128,2048]{2,0,1:T(4,128)} %bitcast.203, f32[1,128,2048]{2,0,1:T(1,128)S(1)} %add.185, s32[]{:T(128)} %constant.137.clone.1, s32[]{:T(128)} %constant.129.clone.1, s32[]{:T(128)} %constant.129.clone.1) | dynamic-update-slice | bytes 2097156 | tf_op jit(solution)/shard_map/scatter-add | solution.py:173
  572.6 2.9 slice_add_fusion
  575.5 19.5 %scatter-add.9 = f32[4,128,2048]{2,0,1:T(4,128)} dynamic-update-slice(f32[4,128,2048]{2,0,1:T(4,128)} %scatter-add.6, f32[1,128,2048]{2,0,1:T(1,128)S(1)} %slice_add_fusion, s32[]{:T(128)} %constant.129.clone.1, s32[]{:T(128)} %constant.129.clone.1, s32[]{:T(128)} %constant.129.clone.1) | dynamic-update-slice | bytes 2097156 | tf_op jit(solution)/shard_map/scatter-add | solution.py:173
  595.0 6.4 fusion.54
  601.4 6.4 fusion.56
  607.9 6.5 fusion.58
  614.4 8.8 %add_convert_fusion = bf16[4,128,2048]{2,0,1:T(4,128)(2,1)} fusion(f32[4,128,2048]{2,0,1:T(4,128)S(1)} %fusion.54, f32[4,128,2048]{2,0,1:T(4,128)S(1)} %fusion.56, f32[4,128,2048]{2,0,1:T(4,128)S(1)} %copy-done, f32[4,128,2048]{2,0,1:T(4,128)S(1)} %fusion.58, f32[2,128,2048]{2,0,1:T(2,128)S(1)} %collective-permute-done.15, pred[4]{0:T(512)(128)(4,1)S(1)} %copy-done.12, ...), kind=kOutput, calls=%fused_computation.41 | convolution fusion | flops 30408720 | bytes 20971540 | tf_op jit(solution)/shard_map/st,sbf->tbf/dot_general | solution.py:177
  623.2 3.5 copy.183
  627.1 39.4 %all_to_all.48 = bf16[4,128,3072]{1,2,0:T(8,128)(2,1)S(1)} all-to-all(bf16[4,128,3072]{1,2,0:T(8,128)(2,1)S(1)} %bitcast.207), channel_id=1, replica_groups=mesh['ctx'=8,'head'=4] {'head'}, dimensions={0} | all-to-all | bytes 6291456 | tf_op jit(solution)/shard_map/all_to_all | solution.py:183
  (202 shorter events, 116.7 us)
Async XLA Ops:
  0.0 23.8 %collective-permute-start.8 = (s32[4,4]{1,0:T(4,128)}, s32[4,4]{1,0:T(4,128)S(1)}, u32[]{:S(2)}, u32[]{:S(2)}) collective-permute-start(s32[4,4]{1,0:T(4,128)} %param.12), channel_id=1, source_target_pairs={{0,8},{4,12},{8,16},{12,20},{16,24},{20,28},{1,9},{5,13},{9,17},{1... | collective-permute-start | bytes 200 | tf_op jit(solution)/shard_map/ppermute | solution.py:34
  5.0 18.9 %collective-permute-start.6 = (s32[4,4]{1,0:T(4,128)}, s32[4,4]{1,0:T(4,128)S(1)}, u32[]{:S(2)}, u32[]{:S(2)}) collective-permute-start(s32[4,4]{1,0:T(4,128)} %param.12), channel_id=1, source_target_pairs={{0,4},{4,8},{8,12},{12,16},{16,20},{20,24},{24,28},{1,5},{5,9},{9,... | collective-permute-start | bytes 200 | tf_op jit(solution)/shard_map/ppermute | solution.py:34
  8.4 15.5 %collective-permute-start.2 = (s32[4,4]{1,0:T(4,128)}, s32[4,4]{1,0:T(4,128)S(1)}, u32[]{:S(2)}, u32[]{:S(2)}) collective-permute-start(s32[4,4]{1,0:T(4,128)} %param.12), channel_id=1, source_target_pairs={{8,0},{12,4},{16,8},{20,12},{24,16},{28,20},{9,1},{13,5},{17,9},{2... | collective-permute-start | bytes 200 | tf_op jit(solution)/shard_map/ppermute | solution.py:34
  9.7 14.2 %collective-permute-start.4 = (s32[4,4]{1,0:T(4,128)}, s32[4,4]{1,0:T(4,128)S(1)}, u32[]{:S(2)}, u32[]{:S(2)}) collective-permute-start(s32[4,4]{1,0:T(4,128)} %param.12), channel_id=1, source_target_pairs={{4,0},{8,4},{12,8},{16,12},{20,16},{24,20},{28,24},{5,1},{9,5},{13... | collective-permute-start | bytes 200 | tf_op jit(solution)/shard_map/ppermute | solution.py:34
  15.6 3.9 copy-start.28
  15.6 6.5 copy-start.10
  15.6 40.7 %all-to-all-start = ((bf16[128,4,3072]{0,2,1:T(8,128)(2,1)}), bf16[128,4,3072]{0,2,1:T(8,128)(2,1)S(1)}, u32[]{:S(2)}, u32[]{:S(2)}) async-start(bf16[128,4,3072]{0,2,1:T(8,128)(2,1)} %bitcast.206), calls=%async_computation | async-start | bytes 6291456 | tf_op jit(solution)/shard_map/all_to_all | solution.py:89
  23.9 79.0 %copy-start.13 = (pred[4]{0:T(512)(128)(4,1)}, pred[4]{0:T(512)(128)(4,1)S(1)}, u32[]{:S(2)}) copy-start(pred[4]{0:T(512)(128)(4,1)S(1)} %get-tuple-element.114) | copy-start | bytes 16
  23.9 88.8 %copy-start.15 = (pred[4]{0:T(512)(128)(4,1)}, pred[4]{0:T(512)(128)(4,1)S(1)}, u32[]{:S(2)}) copy-start(pred[4]{0:T(512)(128)(4,1)S(1)} %get-tuple-element.115) | copy-start | bytes 16
  24.0 95.5 %copy-start.17 = (pred[4]{0:T(512)(128)(4,1)}, pred[4]{0:T(512)(128)(4,1)S(1)}, u32[]{:S(2)}) copy-start(pred[4]{0:T(512)(128)(4,1)S(1)} %get-tuple-element.113) | copy-start | bytes 16
  24.0 99.4 %copy-start.11 = (pred[4]{0:T(512)(128)(4,1)}, pred[4]{0:T(512)(128)(4,1)S(1)}, u32[]{:S(2)}) copy-start(pred[4]{0:T(512)(128)(4,1)S(1)} %get-tuple-element.112) | copy-start | bytes 16
  24.1 78.9 %copy-start.21 = (s32[4]{0:T(128)}, s32[4]{0:T(128)S(1)}, u32[]{:S(2)}) copy-start(s32[4]{0:T(128)S(1)} %get-tuple-element.155) | copy-start | bytes 52
  24.1 88.6 %copy-start.23 = (s32[4]{0:T(128)}, s32[4]{0:T(128)S(1)}, u32[]{:S(2)}) copy-start(s32[4]{0:T(128)S(1)} %get-tuple-element.154) | copy-start | bytes 52
  24.3 95.2 %copy-start.25 = (s32[4]{0:T(128)}, s32[4]{0:T(128)S(1)}, u32[]{:S(2)}) copy-start(s32[4]{0:T(128)S(1)} %get-tuple-element.153) | copy-start | bytes 52
  24.3 99.0 %copy-start.19 = (s32[4]{0:T(128)}, s32[4]{0:T(128)S(1)}, u32[]{:S(2)}) copy-start(s32[4]{0:T(128)S(1)} %get-tuple-element.152) | copy-start | bytes 52
  56.3 136.1 %all-to-all-start.1 = ((bf16[128,4,1024]{0,2,1:T(8,128)(2,1)}), bf16[128,4,1024]{0,2,1:T(8,128)(2,1)}, u32[]{:S(2)}, u32[]{:S(2)}) async-start(bf16[128,4,1024]{0,2,1:T(8,128)(2,1)} %bitcast.211), calls=%async_computation.1 | async-start | bytes 2097152 | tf_op jit(solution)/shard_map/all_to_all | solution.py:90
  80.2 1.7 copy-start.1
  83.1 1.9 copy-start.5
  86.0 10.0 %copy-start.4 = (bf16[128,8,2,128]{0,3,2,1:T(8,128)(2,1)S(1)}, bf16[128,8,2,128]{0,3,2,1:T(8,128)(2,1)}, u32[]{:S(2)}) copy-start(bf16[128,8,2,128]{0,3,2,1:T(8,128)(2,1)} %get-tuple-element.140) | copy-start | bytes 1572868
  86.0 43.1 %collective-permute-start = (bf16[128,2048]{1,0:T(8,128)(2,1)}, bf16[128,2048]{1,0:T(8,128)(2,1)}, u32[]{:S(2)}, u32[]{:S(2)}) collective-permute-start(bf16[128,2048]{1,0:T(8,128)(2,1)} %copy.140), channel_id=1, source_target_pairs={{0,4},{4,8},{8,12},{12,16},{16,20},{20,24},{24,28},{1,5},{5,9},{9,... | collective-permute-start | bytes 1572872 | tf_op jit(solution)/shard_map/ppermute | solution.py:22
  97.0 36.8 %collective-permute-start.1 = (bf16[128,2048]{1,0:T(8,128)(2,1)}, bf16[128,2048]{1,0:T(8,128)(2,1)}, u32[]{:S(2)}, u32[]{:S(2)}) collective-permute-start(bf16[128,2048]{1,0:T(8,128)(2,1)} %copy.141), channel_id=1, source_target_pairs={{4,0},{8,4},{12,8},{16,12},{20,16},{24,20},{28,24},{5,1},{9,5},{13... | collective-permute-start | bytes 1572872 | tf_op jit(solution)/shard_map/ppermute | solution.py:24
  103.0 16.5 %copy-start.3 = (bf16[4,128,2048]{2,0,1:T(4,128)(2,1)}, bf16[4,128,2048]{2,0,1:T(4,128)(2,1)S(1)}, u32[]{:S(2)}) copy-start(bf16[4,128,2048]{2,0,1:T(4,128)(2,1)S(1)} %copy.143) | copy-start | bytes 6291460
  105.6 30.1 %collective-permute-start.3 = (bf16[256,2048]{1,0:T(8,128)(2,1)}, bf16[256,2048]{1,0:T(8,128)(2,1)}, u32[]{:S(2)}, u32[]{:S(2)}) collective-permute-start(bf16[256,2048]{1,0:T(8,128)(2,1)} %bitcast.34), channel_id=1, source_target_pairs={{0,8},{4,12},{8,16},{12,20},{16,24},{20,28},{1,9},{5,13},{9,17},{1... | collective-permute-start | bytes 3145736 | tf_op jit(solution)/shard_map/ppermute | solution.py:34
  115.3 48.3 %collective-permute-start.5 = (bf16[256,2048]{1,0:T(8,128)(2,1)}, bf16[256,2048]{1,0:T(8,128)(2,1)}, u32[]{:S(2)}, u32[]{:S(2)}) collective-permute-start(bf16[256,2048]{1,0:T(8,128)(2,1)} %bitcast.36), channel_id=1, source_target_pairs={{0,4},{4,8},{8,12},{12,16},{16,20},{20,24},{24,28},{1,5},{5,9},{9,... | collective-permute-start | bytes 3145736 | tf_op jit(solution)/shard_map/ppermute | solution.py:34
  120.7 7.0 %slice-start = ((bf16[512,8,3,128]{0,3,2,1:T(8,128)(2,1)}), bf16[512,8,1,128]{0,3,2,1:T(8,128)(2,1)S(1)}, s32[]{:S(2)}) async-start(bf16[512,8,3,128]{0,3,2,1:T(8,128)(2,1)} %copy-done.1), calls=%async_computation.3 | async-start | bytes 2097152 | tf_op jit(solution)/shard_map/slice | solution.py:96
  122.0 43.9 %collective-permute-start.7 = (bf16[256,2048]{1,0:T(8,128)(2,1)}, bf16[256,2048]{1,0:T(8,128)(2,1)}, u32[]{:S(2)}, u32[]{:S(2)}) collective-permute-start(bf16[256,2048]{1,0:T(8,128)(2,1)} %bitcast.38), channel_id=1, source_target_pairs={{4,0},{8,4},{12,8},{16,12},{20,16},{24,20},{28,24},{5,1},{9,5},{13... | collective-permute-start | bytes 3145736 | tf_op jit(solution)/shard_map/ppermute | solution.py:34
  123.3 9.0 %copy-start.2 = (bf16[512,2048]{1,0:T(8,128)(2,1)S(1)}, bf16[512,2048]{1,0:T(8,128)(2,1)}, u32[]{:S(2)}) copy-start(bf16[512,2048]{1,0:T(8,128)(2,1)} %copy.151) | copy-start | bytes 6291460
  129.1 42.2 %collective-permute-start.9 = (bf16[256,2048]{1,0:T(8,128)(2,1)}, bf16[256,2048]{1,0:T(8,128)(2,1)S(1)}, u32[]{:S(2)}, u32[]{:S(2)}) collective-permute-start(bf16[256,2048]{1,0:T(8,128)(2,1)} %bitcast.215), channel_id=1, source_target_pairs={{8,0},{12,4},{16,8},{20,12},{24,16},{28,20},{9,1},{13,5},{17,9},{2... | collective-permute-start | bytes 3145736 | tf_op jit(solution)/shard_map/ppermute | solution.py:34
  185.0 7.5 %copy-start.6 = (bf16[4,128,8,128]{1,3,2,0:T(8,128)(2,1)S(1)}, bf16[4,128,8,128]{1,3,2,0:T(8,128)(2,1)}, u32[]{:S(2)}) copy-start(bf16[4,128,8,128]{1,3,2,0:T(8,128)(2,1)} %custom-call.3) | copy-start | bytes 3145732
  335.7 51.0 %copy-start.7 = (bf16[4,128,8,128]{1,3,2,0:T(8,128)(2,1)}, bf16[4,128,8,128]{1,3,2,0:T(8,128)(2,1)S(1)}, u32[]{:S(2)}) copy-start(bf16[4,128,8,128]{1,3,2,0:T(8,128)(2,1)S(1)} %get-tuple-element.72) | copy-start | bytes 3145732
  335.7 51.0 %copy-start.27 = (s32[28]{0:T(128)S(1)}, s32[28]{0:T(128)}, u32[]{:S(2)}) copy-start(s32[28]{0:T(128)} %eq.235) | copy-start | bytes 340
  427.5 167.4 %collective-permute-start.14 = (f32[2,128,2048]{2,0,1:T(2,128)}, f32[2,128,2048]{2,0,1:T(2,128)}, u32[]{:S(2)}, u32[]{:S(2)}) collective-permute-start(f32[2,128,2048]{2,0,1:T(2,128)} %bitcast.52), channel_id=1, source_target_pairs={{0,4},{4,8},{8,12},{12,16},{16,20},{20,24},{24,28},{1,5},{5,9},{9,... | collective-permute-start | bytes 6291464 | tf_op jit(solution)/shard_map/ppermute | solution.py:34
  430.2 171.2 %collective-permute-start.13 = (f32[2,128,2048]{2,0,1:T(2,128)}, f32[2,128,2048]{2,0,1:T(2,128)}, u32[]{:S(2)}, u32[]{:S(2)}) collective-permute-start(f32[2,128,2048]{2,0,1:T(2,128)} %bitcast.50), channel_id=1, source_target_pairs={{4,0},{8,4},{12,8},{16,12},{20,16},{24,20},{28,24},{5,1},{9,5},{13... | collective-permute-start | bytes 6291464 | tf_op jit(solution)/shard_map/ppermute | solution.py:34
  445.6 45.7 %collective-permute-start.10 = (bf16[128,2048]{1,0:T(8,128)(2,1)S(1)}, bf16[128,2048]{1,0:T(8,128)(2,1)S(1)}, u32[]{:S(2)}, u32[]{:S(2)}) collective-permute-start(bf16[128,2048]{1,0:T(8,128)(2,1)S(1)} %convert_element_type.86), channel_id=1, source_target_pairs={{4,0},{8,4},{12,8},{16,12},{20,16},{24,20},{28,24},{5,1},{9,5},{13... | collective-permute-start | bytes 1572872 | tf_op jit(solution)/shard_map/ppermute | solution.py:34
  447.9 123.5 %collective-permute-start.11 = (bf16[128,2048]{1,0:T(8,128)(2,1)}, bf16[128,2048]{1,0:T(8,128)(2,1)}, u32[]{:S(2)}, u32[]{:S(2)}) collective-permute-start(bf16[128,2048]{1,0:T(8,128)(2,1)} %convert_element_type.88), channel_id=1, source_target_pairs={{0,4},{4,8},{8,12},{12,16},{16,20},{20,24},{24,28},{1,5},{5,9},{9,... | collective-permute-start | bytes 1572872 | tf_op jit(solution)/shard_map/ppermute | solution.py:34
  455.4 152.4 %collective-permute-start.12 = (f32[2,128,2048]{2,0,1:T(2,128)}, f32[2,128,2048]{2,0,1:T(2,128)}, u32[]{:S(2)}, u32[]{:S(2)}) collective-permute-start(f32[2,128,2048]{2,0,1:T(2,128)} %bitcast.48), channel_id=1, source_target_pairs={{8,0},{12,4},{16,8},{20,12},{24,16},{28,20},{9,1},{13,5},{17,9},{2... | collective-permute-start | bytes 6291464 | tf_op jit(solution)/shard_map/ppermute | solution.py:34
  491.3 0.8 copy-start.9
  492.1 122.3 %collective-permute-start.15 = (f32[2,128,2048]{2,0,1:T(2,128)}, f32[2,128,2048]{2,0,1:T(2,128)S(1)}, u32[]{:S(2)}, u32[]{:S(2)}) collective-permute-start(f32[2,128,2048]{2,0,1:T(2,128)} %bitcast.214), channel_id=1, source_target_pairs={{0,8},{4,12},{8,16},{12,20},{16,24},{20,28},{1,9},{5,13},{9,17},{1... | collective-permute-start | bytes 6291464 | tf_op jit(solution)/shard_map/ppermute | solution.py:34
  571.4 23.5 %copy-start.18 = (pred[4]{0:T(512)(128)(4,1)S(1)}, pred[4]{0:T(512)(128)(4,1)}, u32[]{:S(2)}) copy-start(pred[4]{0:T(512)(128)(4,1)} %copy-done.17) | copy-start | bytes 16
  571.4 23.5 %copy-start.26 = (s32[4]{0:T(128)S(1)}, s32[4]{0:T(128)}, u32[]{:S(2)}) copy-start(s32[4]{0:T(128)} %copy-done.25) | copy-start | bytes 52
  594.9 6.5 copy-start.16
  594.9 6.5 copy-start.24
  601.4 6.5 copy-start.14
  601.4 6.5 copy-start.22
  607.8 6.6 copy-start
  607.8 6.6 copy-start.12
  607.8 6.6 copy-start.20
  623.2 3.5 copy-start.8
where the time goes:
time: 681 us; the launch traced here: 670 us
  local copies, waits for them, and re-layouts  318 us (47%)
  starting transfers between devices  111 us (16%)
  matrix products  83.9 us (12%)
  waiting for transfers between devices  76.7 us (11%)
  blocking collectives  39.4 us (6%)
  other arithmetic  38.5 us (6%)
    ppermute x14, starting transfers between devices, from_behind(): lax.ppermute(value, axis, [(source, source + steps) for source in range(i...  96.5 us
    reshape x1, local copies, waits for them, and re-layouts, shards(): flat_terms = pair_terms.reshape(slot_total, BLK * pair_width)  51 us
    dynamic_update_slice x4, local copies, waits for them, and re-layouts, shards(): lax.scan(step, carry_zero, (query_blocks, grad_blocks, places, usable))  46.9 us
    ppermute x14, waiting for transfers between devices, from_behind(): lax.ppermute(value, axis, [(source, source + steps) for source in range(i...  44.7 us
    all_to_all x1, blocking collectives, shards(): lax.all_to_all(joined, 'head', split_axis=0, concat_axis=1, tiled=True)  39.4 us
    scatter-add x2, local copies, waits for them, and re-layouts, shards(): own_grads = own_grads.at[target_block].add(arrived)  39.2 us
    all_to_all x1, waiting for transfers between devices, shards(): lax.all_to_all(qkv, 'head', split_axis=1, concat_axis=0, tiled=True)  32 us
    dot_general x4, matrix products, shards(): jnp.einsum('st,sbf->tbf', owner_tables[side_index], arrived, precision=la...  28.1 us
  transfers between devices with their start and end apart: 18, of which 4 were waited for; matrix products, arithmetic and copies ran while one was open for 28% of the time, Pallas kernels for 0%

commit v1 on v0

--- a/solution.py
+++ b/solution.py
@@ -9,6 +9,28 @@
 DRAWN_TARGET_SET = 4
 SPAN = 2
 NAMED_TILE_LIMIT = 2
+
+
+def plate_recast(in_array):
+    chip_axis = "head"
+    u1 = jax.lax.axis_size(chip_axis)
+    reply, later = (u1, jax.lax.axis_index(chip_axis))
+    all_rows = in_array.shape[1] // reply
+    before = list(in_array.shape)
+    before[1] = all_rows
+    u_next = before[0]
+    before[0] = u_next * reply
+    local_out = jnp.zeros(before, in_array.dtype)
+    for kk in tuple(range(reply)):
+        s_next = lax.dynamic_slice_in_dim(in_array, (later ^ kk) * all_rows, all_rows, axis=1)
+        if kk:
+            s_next = jax.lax.ppermute(
+                s_next, axis_name=chip_axis, perm=[(jj, jj ^ kk) for jj in range(reply)]
+            )
+        local_out = lax.dynamic_update_slice_in_dim(
+            local_out, s_next, (later ^ kk) * u_next, axis=0
+        )
+    return local_out
 
 
 def extended_2(cells, sides, width):
@@ -86,7 +108,7 @@
 
 def shards(qkv, grad_out, key_lists, live_counts):
     merged, grad_rows = (
-        lax.all_to_all(qkv, "head", split_axis=1, concat_axis=0, tiled=True),
+        plate_recast(qkv),
         lax.all_to_all(grad_out, "head", split_axis=1, concat_axis=0, tiled=True),
     )
     row_count = merged.shape[0]

time: 681 us -> 658 us (0.966)
  local copies, waits for them, and re-layouts: 318 us -> 303 us
    all_to_all x1 -> x0, waiting for transfers between devices: 32 us -> none  [shards(): lax.all_to_all(qkv, 'head', split_axis=1, concat_axis=0, tiled=True)]
    ppermute x0 -> x3, waiting for transfers between devices: none -> 25.4 us  [plate_recast(): jax.lax.ppermute(s_next, axis_name=chip_axis, perm=[(jj, jj ^ kk) for jj...]
    all_to_all x1 -> x0, local copies, waits for them, and re-layouts: 15.6 us -> none  [shards(): lax.all_to_all(qkv, 'head', split_axis=1, concat_axis=0, tiled=True)]
    unnamed x66 -> x71, local copies, waits for them, and re-layouts: 21.7 us -> 22.6 us
  transfers between devices with their start and end apart: 18 -> 20, of which waited for: 4 -> 5; matrix products, arithmetic and copies ran while one was open for 28% -> 27% of each run, Pallas kernels for 0% -> 0%
where the time goes in v1:
time: 658 us; the launch traced here: 647 us
  local copies, waits for them, and re-layouts  303 us (46%)
  starting transfers between devices  109 us (17%)
  matrix products  83.8 us (13%)
  waiting for transfers between devices  70.9 us (11%)
  blocking collectives  39.5 us (6%)
  other arithmetic  38.5 us (6%)
    ppermute x14, starting transfers between devices, from_behind(): lax.ppermute(value, axis, [(source, source + steps) for source in range(i...  96 us
    reshape x1, local copies, waits for them, and re-layouts, shards(): flat_terms = pair_terms.reshape(slot_total, BLK * pair_width)  51 us
    dynamic_update_slice x4, local copies, waits for them, and re-layouts, shards(): lax.scan(step, carry_zero, (query_blocks, grad_blocks, places, usable))  46.9 us
    ppermute x14, waiting for transfers between devices, from_behind(): lax.ppermute(value, axis, [(source, source + steps) for source in range(i...  45.5 us
    all_to_all x1, blocking collectives, shards(): lax.all_to_all(joined, 'head', split_axis=0, concat_axis=1, tiled=True)  39.5 us
    scatter-add x2, local copies, waits for them, and re-layouts, shards(): own_grads = own_grads.at[target_block].add(arrived)  39.4 us
    dot_general x4, matrix products, shards(): jnp.einsum('st,sbf->tbf', owner_tables[side_index], arrived, precision=la...  28 us
    dot_general x1, matrix products, shards(): jnp.dot(owner_hits, flat_terms, precision=lax.Precision.HIGHEST, preferre...  25.8 us
  transfers between devices with their start and end apart: 20, of which 5 were waited for; matrix products, arithmetic and copies ran while one was open for 27% of the time, Pallas kernels for 0%

profile of v1, /device:TPU:0, one launch (start us, length us, event | category | flops | bytes accessed | tf_op | source)
XLA Modules:
  0.0 646.7 jit_solution(19459729218762658)
XLA Ops:
  0.0 4.9 collective-permute-start.11
  5.0 3.4 collective-permute-start.9
  17.9 4.2 all-to-all-start
  30.9 2.4 collective-permute-done.7
  36.5 25.4 %collective-permute-done.2 = bf16[128,3072]{0,1:T(8,128)(2,1)S(1)} collective-permute-done((bf16[128,3072]{0,1:T(8,128)(2,1)}, bf16[128,3072]{0,1:T(8,128)(2,1)S(1)}, u32[]{:S(2)}, u32[]{:S(2)}) %collective-permute-start.2) | collective-permute-done | bytes 786464 | tf_op jit(solution)/shard_map/ppermute | solution.py:27
  70.1 4.4 collective-permute-start.3
  76.6 2.4 copy.122
  81.3 4.6 copy.114
  88.5 6.8 %collective-permute-start.6 = (bf16[256,2048]{1,0:T(8,128)(2,1)}, bf16[256,2048]{1,0:T(8,128)(2,1)}, u32[]{:S(2)}, u32[]{:S(2)}) collective-permute-start(bf16[256,2048]{1,0:T(8,128)(2,1)} %bitcast.33), channel_id=1, source_target_pairs={{0,8},{4,12},{8,16},{12,20},{16,24},{20,28},{1,9},{5,13},{9,17},{1... | collective-permute-start | bytes 3145736 | tf_op jit(solution)/shard_map/ppermute | solution.py:56
  97.9 3.5 collective-permute-start.8
  105.8 3.0 convolution_convert_fusion
  120.8 24.4 %collective-permute-done.8 = bf16[256,2048]{1,0:T(8,128)(2,1)} collective-permute-done((bf16[256,2048]{1,0:T(8,128)(2,1)}, bf16[256,2048]{1,0:T(8,128)(2,1)}, u32[]{:S(2)}, u32[]{:S(2)}) %collective-permute-start.8) | collective-permute-done | bytes 1048608 | tf_op jit(solution)/shard_map/ppermute | solution.py:56
  149.9 2.8 collective-permute-done.12
  153.7 12.6 %reshape.225 = bf16[14,128,8,2,128]{4,3,2,1,0:T(2,128)(2,1)} reshape(bf16[1792,2048]{1,0:T(8,128)(2,1)} %constant_dynamic-update-slice_fusion) | data formatting | bytes 14680064 | tf_op jit(solution)/shard_map/reshape | solution.py:163
  166.4 7.5 %copy.125 = bf16[14,128,8,2,128]{4,2,3,1,0:T(8,128)(2,1)} copy(bf16[14,128,8,2,128]{4,3,2,1,0:T(2,128)(2,1)} %reshape.225) | data formatting | bytes 14680064 | tf_op jit(solution)/shard_map/while | solution.py:176
  173.8 139.1 %while.14 = (s32[]{:T(128)}, bf16[4,128,8,128]{1,3,2,0:T(8,128)(2,1)S(1)}, f32[4,7,128,8,2,128]{5,4,3,2,1,0:T(2,128)}, s32[4,7]{1,0:T(4,128)S(1)}, bf16[14,128,8...) while((s32[]{:T(128)}, ...), condition=%wide.region_21.22_spmd, body=%wide.region_17.21_spmd.sunk | while | flops 1203894272 | bytes 104907184 | solution.py:176
  173.8 6.1 gather_fusion
  192.9 3.9 maximum_bitcast_fusion.2
  196.8 11.7 %copy_dynamic-update-slice_fusion.2 = f32[4,7,128,8,2,128]{5,4,3,2,1,0:T(2,128)} fusion(f32[4,7,128,8,2,128]{5,4,3,2,1,0:T(2,128)} %get-tuple-element.220, s32[]{:T(128)S(6)} %copy.205, f32[1,7,128,8,2,128]{5,2,1,3,4,0:T(8,128)} %maximum_bitcast_fusion.2), kind=kLoop, calls=%fused_computation.2.clone.1 | loop fusion | bytes 14680068 | tf_op jit(solution)/shard_map/while/body/jit(dynamic_update_index_in_dim)/dynamic_update_slice | solution.py:176
  208.5 6.1 gather_fusion
  227.6 3.9 maximum_bitcast_fusion.2
  231.5 11.8 %copy_dynamic-update-slice_fusion.2 = f32[4,7,128,8,2,128]{5,4,3,2,1,0:T(2,128)} fusion(f32[4,7,128,8,2,128]{5,4,3,2,1,0:T(2,128)} %get-tuple-element.220, s32[]{:T(128)S(6)} %copy.205, f32[1,7,128,8,2,128]{5,2,1,3,4,0:T(8,128)} %maximum_bitcast_fusion.2), kind=kLoop, calls=%fused_computation.2.clone.1 | loop fusion | bytes 14680068 | tf_op jit(solution)/shard_map/while/body/jit(dynamic_update_index_in_dim)/dynamic_update_slice | solution.py:176
  243.3 6.1 gather_fusion
  262.4 3.9 maximum_bitcast_fusion.2
  266.3 11.8 %copy_dynamic-update-slice_fusion.2 = f32[4,7,128,8,2,128]{5,4,3,2,1,0:T(2,128)} fusion(f32[4,7,128,8,2,128]{5,4,3,2,1,0:T(2,128)} %get-tuple-element.220, s32[]{:T(128)S(6)} %copy.205, f32[1,7,128,8,2,128]{5,2,1,3,4,0:T(8,128)} %maximum_bitcast_fusion.2), kind=kLoop, calls=%fused_computation.2.clone.1 | loop fusion | bytes 14680068 | tf_op jit(solution)/shard_map/while/body/jit(dynamic_update_index_in_dim)/dynamic_update_slice | solution.py:176
  278.1 6.1 gather_fusion
  297.1 3.9 maximum_bitcast_fusion.2
  301.1 11.7 %copy_dynamic-update-slice_fusion.2 = f32[4,7,128,8,2,128]{5,4,3,2,1,0:T(2,128)} fusion(f32[4,7,128,8,2,128]{5,4,3,2,1,0:T(2,128)} %get-tuple-element.220, s32[]{:T(128)S(6)} %copy.205, f32[1,7,128,8,2,128]{5,2,1,3,4,0:T(8,128)} %maximum_bitcast_fusion.2), kind=kLoop, calls=%fused_computation.2.clone.1 | loop fusion | bytes 14680068 | tf_op jit(solution)/shard_map/while/body/jit(dynamic_update_index_in_dim)/dynamic_update_slice | solution.py:176
  312.9 51.0 %reshape.227 = f32[28,262144]{1,0:T(8,128)} reshape(f32[4,7,128,8,2,128]{5,4,3,2,1,0:T(2,128)} %get-tuple-element.73) | data formatting | bytes 58720256 | tf_op jit(solution)/shard_map/reshape | solution.py:179
  363.9 25.8 %fusion.84 = (bf16[14,262144]{1,0:T(8,128)(2,1)}, f32[14,262144]{1,0:T(8,128)}) fusion(f32[28,262144]{1,0:T(8,128)} %reshape.227, s32[28]{0:T(128)S(1)} %copy-done.28), kind=kOutput, calls=%fused_computation.160 | convolution fusion | flops 1236795776 | bytes 51380336 | tf_op jit(solution)/shard_map/dot_general | solution.py:184
  389.6 15.1 %fusion.82 = (f32[2,262144]{1,0:T(2,128)}, f32[2,262144]{1,0:T(2,128)}, f32[2,262144]{1,0:T(2,128)}, f32[2,262144]{1,0:T(2,128)}) fusion(f32[14,262144]{1,0:T(8,128)} %get-tuple-element.141), kind=kLoop, calls=%fused_computation.158 | loop fusion | bytes 16777216 | tf_op jit(solution)/shard_map/slice | solution.py:198
  404.7 2.9 collective-permute-start.17
  409.0 13.9 %slice_reduce_fusion = (bf16[262144]{0:T(1024)(128)(2,1)S(1)}, bf16[262144]{0:T(1024)(128)(2,1)S(1)}) fusion(bf16[14,262144]{1,0:T(8,128)(2,1)} %get-tuple-element.140), kind=kLoop, calls=%fused_computation.47 | loop fusion | bytes 2097152 | tf_op jit(solution)/shard_map/slice | solution.py:190
  425.4 7.2 %collective-permute-start.14 = (bf16[128,2048]{1,0:T(8,128)(2,1)}, bf16[128,2048]{1,0:T(8,128)(2,1)}, u32[]{:S(2)}, u32[]{:S(2)}) collective-permute-start(bf16[128,2048]{1,0:T(8,128)(2,1)} %convert_element_type.88), channel_id=1, source_target_pairs={{0,4},{4,8},{8,12},{12,16},{16,20},{20,24},{24,28},{1,5},{5,9},{9,... | collective-permute-start | bytes 1572872 | tf_op jit(solution)/shard_map/ppermute | solution.py:56
  433.9 13.2 %slice_reduce_fusion.2 = f32[262144]{0:T(1024)S(1)} fusion(f32[14,262144]{1,0:T(8,128)} %get-tuple-element.141), kind=kLoop, calls=%fused_computation.50 | loop fusion | bytes 2097152 | tf_op jit(solution)/shard_map/slice.64
  447.1 5.2 slice.140
  452.5 15.9 %collective-permute-done.13 = bf16[128,2048]{1,0:T(8,128)(2,1)S(1)} collective-permute-done((bf16[128,2048]{1,0:T(8,128)(2,1)S(1)}, bf16[128,2048]{1,0:T(8,128)(2,1)S(1)}, u32[]{:S(2)}, u32[]{:S(2)}) %collective-permute-start.13) | collective-permute-done | bytes 524320 | tf_op jit(solution)/shard_map/ppermute | solution.py:56
  469.2 57.7 %collective-permute-start.18 = (f32[2,128,2048]{2,0,1:T(2,128)}, f32[2,128,2048]{2,0,1:T(2,128)S(1)}, u32[]{:S(2)}, u32[]{:S(2)}) collective-permute-start(f32[2,128,2048]{2,0,1:T(2,128)} %bitcast.211), channel_id=1, source_target_pairs={{0,8},{4,12},{8,16},{12,20},{16,24},{20,28},{1,9},{5,13},{9,17},{1... | collective-permute-start | bytes 6291464 | tf_op jit(solution)/shard_map/ppermute | solution.py:56
  528.8 19.9 %scatter-add.6 = f32[4,128,2048]{2,0,1:T(4,128)} dynamic-update-slice(f32[4,128,2048]{2,0,1:T(4,128)} %bitcast.200, f32[1,128,2048]{2,0,1:T(1,128)S(1)} %add.217, s32[]{:T(128)} %constant.147.clone.1, s32[]{:T(128)} %constant.137.clone.1, s32[]{:T(128)} %constant.137.clone.1) | dynamic-update-slice | bytes 2097156 | tf_op jit(solution)/shard_map/scatter-add | solution.py:195
  549.8 2.9 slice_add_fusion
  552.7 19.5 %scatter-add.9 = f32[4,128,2048]{2,0,1:T(4,128)} dynamic-update-slice(f32[4,128,2048]{2,0,1:T(4,128)} %scatter-add.6, f32[1,128,2048]{2,0,1:T(1,128)S(1)} %slice_add_fusion, s32[]{:T(128)} %constant.137.clone.1, s32[]{:T(128)} %constant.137.clone.1, s32[]{:T(128)} %constant.137.clone.1) | dynamic-update-slice | bytes 2097156 | tf_op jit(solution)/shard_map/scatter-add | solution.py:195
  572.2 6.4 fusion.54
  578.7 6.4 fusion.56
  585.1 6.5 %fusion.58 = f32[4,128,2048]{2,0,1:T(4,128)S(1)} fusion(f32[2,128,2048]{2,0,1:T(2,128)} %collective-permute-done.15, pred[4]{0:T(512)(128)(4,1)S(1)} %copy-done.15, s32[4]{0:T(128)S(1)} %copy-done.23), kind=kOutput, calls=%fused_computation.124 | convolution fusion | flops 25165840 | bytes 6291476 | tf_op jit(solution)/shard_map/st,sbf->tbf/dot_general | solution.py:199
  591.7 8.7 %add_convert_fusion = bf16[4,128,2048]{2,0,1:T(4,128)(2,1)} fusion(f32[4,128,2048]{2,0,1:T(4,128)S(1)} %fusion.54, f32[4,128,2048]{2,0,1:T(4,128)S(1)} %fusion.56, f32[4,128,2048]{2,0,1:T(4,128)S(1)} %copy-done, f32[4,128,2048]{2,0,1:T(4,128)S(1)} %fusion.58, f32[2,128,2048]{2,0,1:T(2,128)S(1)} %collective-permute-done.18, pred[4]{0:T(512)(128)(4,1)S(1)} %copy-done.13, ...), kind=kOutput, calls=%fused_computation.41 | convolution fusion | flops 30408720 | bytes 20971540 | tf_op jit(solution)/shard_map/st,sbf->tbf/dot_general | solution.py:199
  600.4 3.5 copy.154
  604.2 39.5 %all_to_all.32 = bf16[4,128,3072]{1,2,0:T(8,128)(2,1)S(1)} all-to-all(bf16[4,128,3072]{1,2,0:T(8,128)(2,1)S(1)} %bitcast.205), channel_id=1, replica_groups=mesh['ctx'=8,'head'=4] {'head'}, dimensions={0} | all-to-all | bytes 6291456 | tf_op jit(solution)/shard_map/all_to_all | solution.py:205
  643.7 2.8 copy.135
  (214 shorter events, 122.1 us)
Async XLA Ops:
  0.0 27.8 %collective-permute-start.11 = (s32[4,4]{1,0:T(4,128)}, s32[4,4]{1,0:T(4,128)S(1)}, u32[]{:S(2)}, u32[]{:S(2)}) collective-permute-start(s32[4,4]{1,0:T(4,128)} %param.12), channel_id=1, source_target_pairs={{0,8},{4,12},{8,16},{12,20},{16,24},{20,28},{1,9},{5,13},{9,17},{1... | collective-permute-start | bytes 200 | tf_op jit(solution)/shard_map/ppermute | solution.py:56
  5.0 24.2 %collective-permute-start.9 = (s32[4,4]{1,0:T(4,128)}, s32[4,4]{1,0:T(4,128)S(1)}, u32[]{:S(2)}, u32[]{:S(2)}) collective-permute-start(s32[4,4]{1,0:T(4,128)} %param.12), channel_id=1, source_target_pairs={{0,4},{4,8},{8,12},{12,16},{16,20},{20,24},{24,28},{1,5},{5,9},{9,... | collective-permute-start | bytes 200 | tf_op jit(solution)/shard_map/ppermute | solution.py:56
  8.4 22.5 %collective-permute-start.5 = (s32[4,4]{1,0:T(4,128)}, s32[4,4]{1,0:T(4,128)S(1)}, u32[]{:S(2)}, u32[]{:S(2)}) collective-permute-start(s32[4,4]{1,0:T(4,128)} %param.12), channel_id=1, source_target_pairs={{8,0},{12,4},{16,8},{20,12},{24,16},{28,20},{9,1},{13,5},{17,9},{2... | collective-permute-start | bytes 200 | tf_op jit(solution)/shard_map/ppermute | solution.py:56
  11.7 10.4 %copy-start.11 = (s32[4,4]{1,0:T(4,128)S(1)}, s32[4,4]{1,0:T(4,128)}, u32[]{:S(2)}) copy-start(s32[4,4]{1,0:T(4,128)} %param.12) | copy-start | bytes 196
  12.9 20.9 %collective-permute-start = (bf16[128,3072]{0,1:T(8,128)(2,1)}, bf16[128,3072]{0,1:T(8,128)(2,1)}, u32[]{:S(2)}, u32[]{:S(2)}) collective-permute-start(bf16[128,3072]{0,1:T(8,128)(2,1)} %copy.162), channel_id=1, source_target_pairs={{0,1},{1,0},{2,3},{3,2},{4,5},{5,4},{6,7},{7,6},{8,9},{9,8},{10,11... | collective-permute-start | bytes 2359304 | tf_op jit(solution)/shard_map/ppermute | solution.py:27
  14.1 11.6 %copy-start.29 = (s32[4]{0:T(128)S(1)}, s32[4]{0:T(128)}, u32[]{:S(2)}) copy-start(s32[4]{0:T(128)} %param.13) | copy-start | bytes 52
  14.1 21.1 %collective-permute-start.1 = (bf16[128,3072]{0,1:T(8,128)(2,1)}, bf16[128,3072]{0,1:T(8,128)(2,1)}, u32[]{:S(2)}, u32[]{:S(2)}) collective-permute-start(bf16[128,3072]{0,1:T(8,128)(2,1)} %copy.163), channel_id=1, source_target_pairs={{0,2},{1,3},{2,0},{3,1},{4,6},{5,7},{6,4},{7,5},{8,10},{9,11},{10,... | collective-permute-start | bytes 2359304 | tf_op jit(solution)/shard_map/ppermute | solution.py:27
  17.9 155.9 %all-to-all-start = ((bf16[128,4,1024]{0,2,1:T(8,128)(2,1)}), bf16[128,4,1024]{0,2,1:T(8,128)(2,1)}, u32[]{:S(2)}, u32[]{:S(2)}) async-start(bf16[128,4,1024]{0,2,1:T(8,128)(2,1)} %bitcast.41), calls=%async_computation | async-start | bytes 2097152 | tf_op jit(solution)/shard_map/all_to_all | solution.py:112
  27.8 5.5 collective-permute-start.7
  29.1 32.7 %collective-permute-start.2 = (bf16[128,3072]{0,1:T(8,128)(2,1)}, bf16[128,3072]{0,1:T(8,128)(2,1)S(1)}, u32[]{:S(2)}, u32[]{:S(2)}) collective-permute-start(bf16[128,3072]{0,1:T(8,128)(2,1)} %copy.164), channel_id=1, source_target_pairs={{0,3},{1,2},{2,1},{3,0},{4,7},{5,6},{6,5},{7,4},{8,11},{9,10},{10,... | collective-permute-start | bytes 2359304 | tf_op jit(solution)/shard_map/ppermute | solution.py:27
  33.4 52.5 %copy-start.14 = (pred[4]{0:T(512)(128)(4,1)}, pred[4]{0:T(512)(128)(4,1)S(1)}, u32[]{:S(2)}) copy-start(pred[4]{0:T(512)(128)(4,1)S(1)} %get-tuple-element.106) | copy-start | bytes 16
  33.4 61.9 %copy-start.16 = (pred[4]{0:T(512)(128)(4,1)}, pred[4]{0:T(512)(128)(4,1)S(1)}, u32[]{:S(2)}) copy-start(pred[4]{0:T(512)(128)(4,1)S(1)} %get-tuple-element.107) | copy-start | bytes 16
  33.4 68.0 %copy-start.18 = (pred[4]{0:T(512)(128)(4,1)}, pred[4]{0:T(512)(128)(4,1)S(1)}, u32[]{:S(2)}) copy-start(pred[4]{0:T(512)(128)(4,1)S(1)} %get-tuple-element.105) | copy-start | bytes 16
  33.4 72.3 %copy-start.12 = (pred[4]{0:T(512)(128)(4,1)}, pred[4]{0:T(512)(128)(4,1)S(1)}, u32[]{:S(2)}) copy-start(pred[4]{0:T(512)(128)(4,1)S(1)} %get-tuple-element.104) | copy-start | bytes 16
  33.6 52.3 %copy-start.22 = (s32[4]{0:T(128)}, s32[4]{0:T(128)S(1)}, u32[]{:S(2)}) copy-start(s32[4]{0:T(128)S(1)} %get-tuple-element.145) | copy-start | bytes 52
  33.6 61.7 %copy-start.24 = (s32[4]{0:T(128)}, s32[4]{0:T(128)S(1)}, u32[]{:S(2)}) copy-start(s32[4]{0:T(128)S(1)} %get-tuple-element.144) | copy-start | bytes 52
  33.8 67.6 %copy-start.26 = (s32[4]{0:T(128)}, s32[4]{0:T(128)S(1)}, u32[]{:S(2)}) copy-start(s32[4]{0:T(128)S(1)} %get-tuple-element.143) | copy-start | bytes 52
  33.8 72.0 %copy-start.20 = (s32[4]{0:T(128)}, s32[4]{0:T(128)S(1)}, u32[]{:S(2)}) copy-start(s32[4]{0:T(128)S(1)} %get-tuple-element.142) | copy-start | bytes 52
  62.1 1.7 copy-start.1
  65.0 4.1 copy-start.6
  70.1 8.9 %copy-start.5 = (bf16[128,8,2,128]{0,3,2,1:T(8,128)(2,1)S(1)}, bf16[128,8,2,128]{0,3,2,1:T(8,128)(2,1)}, u32[]{:S(2)}) copy-start(bf16[128,8,2,128]{0,3,2,1:T(8,128)(2,1)} %get-tuple-element.132) | copy-start | bytes 1572868
  70.1 41.8 %collective-permute-start.3 = (bf16[128,2048]{1,0:T(8,128)(2,1)}, bf16[128,2048]{1,0:T(8,128)(2,1)}, u32[]{:S(2)}, u32[]{:S(2)}) collective-permute-start(bf16[128,2048]{1,0:T(8,128)(2,1)} %copy.111), channel_id=1, source_target_pairs={{0,4},{4,8},{8,12},{12,16},{16,20},{20,24},{24,28},{1,5},{5,9},{9,... | collective-permute-start | bytes 1572872 | tf_op jit(solution)/shard_map/ppermute | solution.py:44
  80.0 36.6 %collective-permute-start.4 = (bf16[128,2048]{1,0:T(8,128)(2,1)}, bf16[128,2048]{1,0:T(8,128)(2,1)}, u32[]{:S(2)}, u32[]{:S(2)}) collective-permute-start(bf16[128,2048]{1,0:T(8,128)(2,1)} %copy.112), channel_id=1, source_target_pairs={{4,0},{8,4},{12,8},{16,12},{20,16},{24,20},{28,24},{5,1},{9,5},{13... | collective-permute-start | bytes 1572872 | tf_op jit(solution)/shard_map/ppermute | solution.py:46
  85.9 15.5 %copy-start.4 = (bf16[4,128,2048]{2,0,1:T(4,128)(2,1)}, bf16[4,128,2048]{2,0,1:T(4,128)(2,1)S(1)}, u32[]{:S(2)}) copy-start(bf16[4,128,2048]{2,0,1:T(4,128)(2,1)S(1)} %copy.114) | copy-start | bytes 6291460
  88.5 30.0 %collective-permute-start.6 = (bf16[256,2048]{1,0:T(8,128)(2,1)}, bf16[256,2048]{1,0:T(8,128)(2,1)}, u32[]{:S(2)}, u32[]{:S(2)}) collective-permute-start(bf16[256,2048]{1,0:T(8,128)(2,1)} %bitcast.33), channel_id=1, source_target_pairs={{0,8},{4,12},{8,16},{12,20},{16,24},{20,28},{1,9},{5,13},{9,17},{1... | collective-permute-start | bytes 3145736 | tf_op jit(solution)/shard_map/ppermute | solution.py:56
  97.9 47.4 %collective-permute-start.8 = (bf16[256,2048]{1,0:T(8,128)(2,1)}, bf16[256,2048]{1,0:T(8,128)(2,1)}, u32[]{:S(2)}, u32[]{:S(2)}) collective-permute-start(bf16[256,2048]{1,0:T(8,128)(2,1)} %bitcast.35), channel_id=1, source_target_pairs={{0,4},{4,8},{8,12},{12,16},{16,20},{20,24},{24,28},{1,5},{5,9},{9,... | collective-permute-start | bytes 3145736 | tf_op jit(solution)/shard_map/ppermute | solution.py:56
  104.0 43.5 %collective-permute-start.10 = (bf16[256,2048]{1,0:T(8,128)(2,1)}, bf16[256,2048]{1,0:T(8,128)(2,1)}, u32[]{:S(2)}, u32[]{:S(2)}) collective-permute-start(bf16[256,2048]{1,0:T(8,128)(2,1)} %bitcast.37), channel_id=1, source_target_pairs={{4,0},{8,4},{12,8},{16,12},{20,16},{24,20},{28,24},{5,1},{9,5},{13... | collective-permute-start | bytes 3145736 | tf_op jit(solution)/shard_map/ppermute | solution.py:56
  105.8 9.3 %copy-start.2 = (bf16[512,2048]{1,0:T(8,128)(2,1)S(1)}, bf16[512,2048]{1,0:T(8,128)(2,1)}, u32[]{:S(2)}) copy-start(bf16[512,2048]{1,0:T(8,128)(2,1)} %copy.122) | copy-start | bytes 6291460
  111.9 40.8 %collective-permute-start.12 = (bf16[256,2048]{1,0:T(8,128)(2,1)}, bf16[256,2048]{1,0:T(8,128)(2,1)S(1)}, u32[]{:S(2)}, u32[]{:S(2)}) collective-permute-start(bf16[256,2048]{1,0:T(8,128)(2,1)} %bitcast.212), channel_id=1, source_target_pairs={{8,0},{12,4},{16,8},{20,12},{24,16},{28,20},{9,1},{13,5},{17,9},{2... | collective-permute-start | bytes 3145736 | tf_op jit(solution)/shard_map/ppermute | solution.py:56
  166.3 7.5 %copy-start.7 = (bf16[4,128,8,128]{1,3,2,0:T(8,128)(2,1)S(1)}, bf16[4,128,8,128]{1,3,2,0:T(8,128)(2,1)}, u32[]{:S(2)}) copy-start(bf16[4,128,8,128]{1,3,2,0:T(8,128)(2,1)} %custom-call.3) | copy-start | bytes 3145732
  312.9 51.0 %copy-start.8 = (bf16[4,128,8,128]{1,3,2,0:T(8,128)(2,1)}, bf16[4,128,8,128]{1,3,2,0:T(8,128)(2,1)S(1)}, u32[]{:S(2)}) copy-start(bf16[4,128,8,128]{1,3,2,0:T(8,128)(2,1)S(1)} %get-tuple-element.72) | copy-start | bytes 3145732
  312.9 51.0 %copy-start.28 = (s32[28]{0:T(128)S(1)}, s32[28]{0:T(128)}, u32[]{:S(2)}) copy-start(s32[28]{0:T(128)} %eq.235) | copy-start | bytes 340
  404.7 167.5 %collective-permute-start.17 = (f32[2,128,2048]{2,0,1:T(2,128)}, f32[2,128,2048]{2,0,1:T(2,128)}, u32[]{:S(2)}, u32[]{:S(2)}) collective-permute-start(f32[2,128,2048]{2,0,1:T(2,128)} %bitcast.51), channel_id=1, source_target_pairs={{0,4},{4,8},{8,12},{12,16},{16,20},{20,24},{24,28},{1,5},{5,9},{9,... | collective-permute-start | bytes 6291464 | tf_op jit(solution)/shard_map/ppermute | solution.py:56
  407.7 171.0 %collective-permute-start.16 = (f32[2,128,2048]{2,0,1:T(2,128)}, f32[2,128,2048]{2,0,1:T(2,128)}, u32[]{:S(2)}, u32[]{:S(2)}) collective-permute-start(f32[2,128,2048]{2,0,1:T(2,128)} %bitcast.49), channel_id=1, source_target_pairs={{4,0},{8,4},{12,8},{16,12},{20,16},{24,20},{28,24},{5,1},{9,5},{13... | collective-permute-start | bytes 6291464 | tf_op jit(solution)/shard_map/ppermute | solution.py:56
  423.1 45.3 %collective-permute-start.13 = (bf16[128,2048]{1,0:T(8,128)(2,1)S(1)}, bf16[128,2048]{1,0:T(8,128)(2,1)S(1)}, u32[]{:S(2)}, u32[]{:S(2)}) collective-permute-start(bf16[128,2048]{1,0:T(8,128)(2,1)S(1)} %convert_element_type.86), channel_id=1, source_target_pairs={{4,0},{8,4},{12,8},{16,12},{20,16},{24,20},{28,24},{5,1},{9,5},{13... | collective-permute-start | bytes 1572872 | tf_op jit(solution)/shard_map/ppermute | solution.py:56
  425.4 123.3 %collective-permute-start.14 = (bf16[128,2048]{1,0:T(8,128)(2,1)}, bf16[128,2048]{1,0:T(8,128)(2,1)}, u32[]{:S(2)}, u32[]{:S(2)}) collective-permute-start(bf16[128,2048]{1,0:T(8,128)(2,1)} %convert_element_type.88), channel_id=1, source_target_pairs={{0,4},{4,8},{8,12},{12,16},{16,20},{20,24},{24,28},{1,5},{5,9},{9,... | collective-permute-start | bytes 1572872 | tf_op jit(solution)/shard_map/ppermute | solution.py:56
  432.6 152.5 %collective-permute-start.15 = (f32[2,128,2048]{2,0,1:T(2,128)}, f32[2,128,2048]{2,0,1:T(2,128)}, u32[]{:S(2)}, u32[]{:S(2)}) collective-permute-start(f32[2,128,2048]{2,0,1:T(2,128)} %bitcast.47), channel_id=1, source_target_pairs={{8,0},{12,4},{16,8},{20,12},{24,16},{28,20},{9,1},{13,5},{17,9},{2... | collective-permute-start | bytes 6291464 | tf_op jit(solution)/shard_map/ppermute | solution.py:56
  469.2 122.5 %collective-permute-start.18 = (f32[2,128,2048]{2,0,1:T(2,128)}, f32[2,128,2048]{2,0,1:T(2,128)S(1)}, u32[]{:S(2)}, u32[]{:S(2)}) collective-permute-start(f32[2,128,2048]{2,0,1:T(2,128)} %bitcast.211), channel_id=1, source_target_pairs={{0,8},{4,12},{8,16},{12,20},{16,24},{20,28},{1,9},{5,13},{9,17},{1... | collective-permute-start | bytes 6291464 | tf_op jit(solution)/shard_map/ppermute | solution.py:56
  548.7 23.5 %copy-start.19 = (pred[4]{0:T(512)(128)(4,1)S(1)}, pred[4]{0:T(512)(128)(4,1)}, u32[]{:S(2)}) copy-start(pred[4]{0:T(512)(128)(4,1)} %copy-done.18) | copy-start | bytes 16
  548.7 23.5 %copy-start.27 = (s32[4]{0:T(128)S(1)}, s32[4]{0:T(128)}, u32[]{:S(2)}) copy-start(s32[4]{0:T(128)} %copy-done.26) | copy-start | bytes 52
  572.2 6.5 copy-start.17
  572.2 6.5 copy-start.25
  578.6 6.5 %copy-start.15 = (pred[4]{0:T(512)(128)(4,1)S(1)}, pred[4]{0:T(512)(128)(4,1)}, u32[]{:S(2)}) copy-start(pred[4]{0:T(512)(128)(4,1)} %copy-done.14) | copy-start | bytes 16
  578.6 6.5 %copy-start.23 = (s32[4]{0:T(128)S(1)}, s32[4]{0:T(128)}, u32[]{:S(2)}) copy-start(s32[4]{0:T(128)} %copy-done.22) | copy-start | bytes 52
  585.1 6.6 %copy-start = (f32[4,128,2048]{2,0,1:T(4,128)S(1)}, f32[4,128,2048]{2,0,1:T(4,128)}, u32[]{:S(2)}) copy-start(f32[4,128,2048]{2,0,1:T(4,128)} %scatter-add.9) | copy-start | bytes 12582916
  585.1 6.6 %copy-start.13 = (pred[4]{0:T(512)(128)(4,1)S(1)}, pred[4]{0:T(512)(128)(4,1)}, u32[]{:S(2)}) copy-start(pred[4]{0:T(512)(128)(4,1)} %copy-done.12) | copy-start | bytes 16
  585.1 6.6 %copy-start.21 = (s32[4]{0:T(128)S(1)}, s32[4]{0:T(128)}, u32[]{:S(2)}) copy-start(s32[4]{0:T(128)} %copy-done.20) | copy-start | bytes 52
  600.4 3.5 copy-start.9
  (2 other events, 1.9 us)
